TPU v7x, 256 devices: a whole 4x4x8 slice. The times are simulated.
256 devices in a mesh: row: 32 (over y, z), col: 8 (over x, core).
Axes of the slice: x: 4, y: 4, z: 8, core: 2. Of those that a mesh axis runs over, the one named last changes fastest.
Arguments:
- panel: float32 [8, 32, 256, 256], P(None, 'row', None, 'col'), may hold values from -0.1875 to 0.1875
- slab: bfloat16 [8, 32, 256, 4, 8, 256], P(None, 'row', None, None, 'col'), may hold values from -6 to 6
- cotangent: bfloat16 [8, 32, 256, 4, 8, 256], P(None, 'row', None, None, 'col'), may hold values from -0.0625 to 0.0625
- inverse: float32 [256, 256], replicated, may hold values from -2 to 8, as said below
Outputs:
- updated: bfloat16 [8, 32, 256, 4, 8, 256], P(None, 'row', None, None, 'col')
- grad_panel: float32 [8, 32, 256, 256], P(None, 'row', None, 'col')
- grad_inverse: float32 [256, 256], P(None, 'col')
Inputs may be any that keep to these rules, and one draw needn't show every extreme that they name: `inverse`: lower triangular; diagonal entries between 4 and 8.
All inputs are finite; a program needn't handle non-finite values.
Results may differ from a plain program's by a relative error of at most 0.015.
Values may be sent and summed in bfloat16 or wider, within the bound.
A program may use at most 128 MiB of HBM per device.

v0:
```python
import jax
import jax.numpy as jnp
from jax import lax
from jax.sharding import PartitionSpec as P


def per_device(panel, slab, cotangent, inverse):
    tiles_local = panel.shape[0]
    tile_size = panel.shape[2]
    strip_width = panel.shape[3]
    slab_tiles = slab.shape[3]
    row_count = tiles_local * tile_size
    slab_width = slab_tiles * tile_size
    row_devices = lax.axis_size("row")
    col_devices = lax.axis_size("col")
    row_index = lax.axis_index("row")
    col_index = lax.axis_index("col")
    highest = lax.Precision.HIGHEST
    contract_rows = (((0,), (0,)), ((), ()))
    panel_rows = panel.reshape(row_count, strip_width)
    gathered = lax.all_gather(panel_rows, "col", axis=1, tiled=True)
    factor = jnp.dot(gathered, inverse.T, precision=highest, preferred_element_type=jnp.float32)
    rounded = factor.astype(jnp.bfloat16)
    factor_tiles = rounded.reshape(tiles_local, tile_size, tile_size)
    tile_list = []
    for column_slot in range(slab_tiles):
        tile_index = column_slot * col_devices + col_index
        is_owner = tile_index % row_devices == row_index
        owned_tile = lax.dynamic_index_in_dim(
            factor_tiles, tile_index // row_devices, 0, keepdims=False
        )
        tile_list.append(jnp.where(is_owner, owned_tile, jnp.zeros_like(owned_tile)))
    stacked = jnp.stack(tile_list).reshape(slab_width, tile_size)
    slab_factor = lax.psum(stacked, "row").astype(jnp.float32).astype(jnp.bfloat16)
    slab_rows = slab.reshape(row_count, slab_width)
    product = jnp.dot(rounded, slab_factor.T, preferred_element_type=jnp.float32)
    updated = (slab_rows.astype(jnp.float32) - product).astype(jnp.bfloat16)
    cot_rows = cotangent.reshape(row_count, slab_width)
    factor_grad = -jnp.dot(cot_rows, slab_factor, preferred_element_type=jnp.float32)
    slab_grad = -lax.dot_general(
        cot_rows, rounded, contract_rows, preferred_element_type=jnp.float32
    )
    slab_grad = lax.psum(slab_grad.astype(jnp.bfloat16), "row").astype(jnp.float32)
    grad_tiles = factor_grad.reshape(tiles_local, tile_size, tile_size)
    for column_slot in range(slab_tiles):
        tile_index = column_slot * col_devices + col_index
        is_owner = tile_index % row_devices == row_index
        local_slot = tile_index // row_devices
        current_tile = lax.dynamic_index_in_dim(grad_tiles, local_slot, 0, keepdims=True)
        added_tile = jnp.where(
            is_owner, slab_grad[column_slot * tile_size : (column_slot + 1) * tile_size], 0.0
        )
        grad_tiles = lax.dynamic_update_index_in_dim(
            grad_tiles, current_tile + added_tile[None], local_slot, 0
        )
    factor_grad = grad_tiles.reshape(row_count, tile_size)
    grad_total = lax.psum(factor_grad, "col")
    inverse_strip = lax.dynamic_slice_in_dim(inverse, col_index * strip_width, strip_width, 1)
    grad_panel = jnp.dot(
        grad_total, inverse_strip, precision=highest, preferred_element_type=jnp.float32
    )
    inverse_term = lax.dot_general(
        grad_total, panel_rows, contract_rows, precision=highest, preferred_element_type=jnp.float32
    )
    grad_inverse = lax.psum(inverse_term, "row")
    return (updated.reshape(slab.shape), grad_panel.reshape(panel.shape), grad_inverse)


def solution(mesh):
    in_specs = (
        P(None, "row", None, "col"),
        P(None, "row", None, None, "col", None),
        P(None, "row", None, None, "col", None),
        P(),
    )
    out_specs = (
        P(None, "row", None, None, "col", None),
        P(None, "row", None, "col"),
        P(None, "col"),
    )
    return jax.shard_map(
        per_device, mesh=mesh, in_specs=in_specs, out_specs=out_specs, check_vma=False
    )
```

profile of v0, /device:TPU:0, one launch (start us, length us, event | category | flops | bytes accessed | tf_op | source)
XLA Modules:
  0.0 430.0 jit_solution(7106329265095890)
XLA Ops:
  7.2 0.0 copy-start
  7.2 0.0 all-gather.2.cloned.1.call-start
  7.2 1.7 copy.19
  8.9 0.0 all-gather.2.cloned.1.call-update
  9.0 0.0 all-reduce.6.cloned.1.call-start
  9.1 5.2 %copy.20 = bf16[256,8,4,256]{3,1,2,0:T(8,128)(2,1)} copy(bf16[256,8,4,256]{3,2,1,0:T(4,128)(2,1)} %bitcast.71) | data formatting | bytes 8388608
  14.3 24.5 %all-gather.2.cloned.1.call-done = f32[2048,256]{0,1:T(8,128)} async-done(((f32[2048,32]{0,1:T(8,128)}), f32[2048,256]{0,1:T(8,128)}) %all-gather.2.cloned.1.call-update) | async-done | bytes 2097168 | tf_op jit(solution)/shard_map/all_gather | solution.py:21
  38.8 0.0 copy-done
  38.8 5.0 %convolution_convert_fusion = bf16[2048,256]{1,0:T(8,128)(2,1)S(1)} fusion(f32[2048,256]{0,1:T(8,128)} %all-gather.2.cloned.1.call-done, f32[256,256]{1,0:T(8,128)S(1)} %copy-done), kind=kOutput, calls=%fused_computation.2 | convolution fusion | flops 1611137024 | bytes 3407872 | tf_op jit(solution)/shard_map/dot_general | solution.py:22
  43.9 4.3 fusion.1
  48.2 0.9 pad_maximum_fusion
  49.1 0.0 all-reduce.6.cloned.1.call-update
  49.1 0.2 all-reduce.4.cloned.1.call-start
  49.3 150.0 %all-reduce.6.cloned.1.call-done = (bf16[1024,256]{1,0:T(8,128)(2,1)}, bf16[1024,256]{0,1:T(8,128)(2,1)}) async-done(((bf16[1024,256]{1,0:T(8,128)(2,1)}, bf16[1024,256]{0,1:T(8,128)(2,1)}), (bf16[1024,256]{1,0:T(8,128)(2,1)}, bf16[1024,256]{0,1:T(8,128)(2,1)})) %all-reduce.6.cloned.1.call-update) | async-done | bytes 1048592 | tf_op jit(solution)/shard_map/psum | solution.py:34
  199.3 3.7 convolution_negate_fusion
  202.9 0.0 copy-start.4
  202.9 0.2 copy.24
  203.1 0.9 copy-done.4
  204.0 0.1 convert_element_type.29
  204.1 0.1 fusion.13
  204.2 0.1 fusion.10
  204.2 0.1 fusion.7
  204.3 0.1 fusion.4
  204.4 1.8 copy.14
  206.2 0.0 all-reduce.4.cloned.1.call-update
  206.2 0.0 copy-start.3
  206.2 7.0 %copy.18 = f32[256,8,4,256]{3,1,2,0:T(8,128)} copy(bf16[256,8,4,256]{3,2,1,0:T(4,128)(2,1)} %bitcast.70) | data formatting | bytes 12582912
  213.2 0.0 copy-done.3
  213.2 6.8 %subtract_convert_fusion = bf16[2048,1024]{1,0:T(8,128)(2,1)} fusion(f32[2048,1024]{1,0:T(8,128)} %bitcast.66, bf16[2048,256]{1,0:T(8,128)(2,1)S(1)} %convolution_convert_fusion, bf16[1024,256]{1,0:T(8,128)(2,1)S(1)} %copy-done.3), kind=kOutput, calls=%fused_computation | convolution fusion | flops 1077936128 | bytes 14155776 | tf_op jit(solution)/shard_map/dot_general | solution.py:36
  220.1 7.9 %reshape.36 = bf16[8,1,256,4,1,256]{5,3,2,0,4,1:T(4,128)(2,1)} reshape(bf16[2048,1024]{1,0:T(8,128)(2,1)} %subtract_convert_fusion) | data formatting | bytes 8388608 | tf_op jit(solution)/shard_map/reshape | solution.py:66
  227.9 0.0 copy-start.2
  227.9 46.6 %all-reduce.4.cloned.1.call-done = f32[2048,256]{1,0:T(8,128)} async-done(((f32[2048,256]{1,0:T(8,128)}), f32[2048,256]{1,0:T(8,128)}) %all-reduce.4.cloned.1.call-update) | async-done | bytes 2097168 | tf_op jit(solution)/shard_map/psum | solution.py:57
  274.5 0.0 copy-start.1
  274.5 3.8 fusion.14
  278.3 0.1 copy.21
  278.4 0.8 copy.16
  279.2 0.0 copy-done.2
  279.2 0.0 copy-done.1
  279.2 1.2 fusion.17
  280.4 143.1 %psum.31 = f32[256,32]{0,1:T(8,128)} all-reduce(f32[256,32]{0,1:T(8,128)S(1)} %fusion.17), channel_id=1, replica_groups=mesh['row'=32,'col'=8] {'row'}, use_global_device_ids=true, to_apply=%region_3.4 | all-reduce | flops 8192 | bytes 65536 | tf_op jit(solution)/shard_map/psum | solution.py:65
  (1 shorter events, 0.0 us)
Async XLA Ops:
  7.2 31.7 %copy-start = (f32[256,256]{1,0:T(8,128)S(1)}, f32[256,256]{1,0:T(8,128)}, u32[]{:S(2)}) copy-start(f32[256,256]{1,0:T(8,128)} %param.7) | copy-start | bytes 786436
  7.2 31.7 %all-gather.2.cloned.1.call-start = ((), (), s32[]{:S(2)}) async-start(), calls=%async_computation | async-start | bytes 2359296 | tf_op jit(solution)/shard_map/all_gather | solution.py:21
  9.0 190.3 %all-reduce.6.cloned.1.call-start = ((), (), s32[]{:S(2)}) async-start(), calls=%async_computation.2 | async-start | bytes 2097152 | tf_op jit(solution)/shard_map/psum | solution.py:34
  49.1 225.4 %all-reduce.4.cloned.1.call-start = ((), (), s32[]{:S(2)}) async-start(), calls=%async_computation.1 | async-start | bytes 4194304 | tf_op jit(solution)/shard_map/psum | solution.py:57
  202.9 1.0 copy-start.4
  206.2 7.0 %copy-start.3 = (bf16[1024,256]{1,0:T(8,128)(2,1)S(1)}, bf16[1024,256]{1,0:T(8,128)(2,1)}, u32[]{:S(2)}) copy-start(bf16[1024,256]{1,0:T(8,128)(2,1)} %get-tuple-element.9) | copy-start | bytes 1572868
  227.9 51.3 %copy-start.2 = (f32[4,8,8,256]{3,1,2,0:T(8,128)S(1)}, f32[4,8,8,256]{3,1,2,0:T(8,128)}, u32[]{:S(2)}) copy-start(f32[4,8,8,256]{3,1,2,0:T(8,128)} %copy.19) | copy-start | bytes 786436
  274.5 4.7 %copy-start.1 = (f32[2048,256]{1,0:T(8,128)S(1)}, f32[2048,256]{1,0:T(8,128)}, u32[]{:S(2)}) copy-start(f32[2048,256]{1,0:T(8,128)} %all-reduce.4.cloned.1.call-done) | copy-start | bytes 6291460
Sparse Core Ops, SparseCore 0:
  9.9 28.9 all-gather.1
  49.2 150.0 all-reduce.5
  206.3 68.1 all-reduce.3
where the time goes:
time: 431 us; the launch traced here: 430 us
  waiting for transfers between devices  221 us (51%)
  blocking collectives  143 us (33%)
  local copies, waits for them, and re-layouts  25.5 us (6%)
  matrix products  24.8 us (6%)
  between operations  13.9 us (3%)
    psum x1, waiting for transfers between devices, per_device(): lax.psum(stacked, 'row').astype(jnp.float32).astype(jnp.bfloat16)  150 us
    psum x1, blocking collectives, per_device(): grad_inverse = lax.psum(inverse_term, 'row')  143 us
    psum x1, waiting for transfers between devices, per_device(): grad_total = lax.psum(factor_grad, 'col')  46.6 us
    all_gather x1, waiting for transfers between devices, per_device(): gathered = lax.all_gather(panel_rows, 'col', axis=1, tiled=True)  24.5 us
    unnamed x15, local copies, waits for them, and re-layouts  15.7 us
  transfers between devices with their start and end apart: 3, of which 3 were waited for; matrix products, arithmetic and copies ran while one was open for 6% of the time, Pallas kernels for 0%

commit v1 on v0

--- a/solution.py
+++ b/solution.py
@@ -54,7 +54,7 @@
             grad_tiles, current_tile + added_tile[None], local_slot, 0
         )
     factor_grad = grad_tiles.reshape(row_count, tile_size)
-    grad_total = lax.psum(factor_grad, "col")
+    grad_total = jnp.sum(lax.all_gather(factor_grad, "col"), 0)
     inverse_strip = lax.dynamic_slice_in_dim(inverse, col_index * strip_width, strip_width, 1)
     grad_panel = jnp.dot(
         grad_total, inverse_strip, precision=highest, preferred_element_type=jnp.float32

time: 431 us -> 455 us (1.056)
  waiting for transfers between devices: 221 us -> 237 us
  other arithmetic: 1.27 us -> 8.4 us
    all_gather x0 -> x1, waiting for transfers between devices: none -> 62.4 us  [per_device(): grad_total = jnp.sum(lax.all_gather(factor_grad, 'col'), 0)]
    psum x1 -> x0, waiting for transfers between devices: 46.6 us -> none  [per_device(): grad_total = lax.psum(factor_grad, 'col')]
    reduce_sum x0 -> x1, other arithmetic: none -> 7.14 us  [per_device(): grad_total = jnp.sum(lax.all_gather(factor_grad, 'col'), 0)]
    unnamed x15 -> x11, local copies, waits for them, and re-layouts: 15.7 us -> 14.8 us
where the time goes in v1:
time: 455 us; the launch traced here: 453 us
  waiting for transfers between devices  237 us (52%)
  blocking collectives  143 us (31%)
  local copies, waits for them, and re-layouts  24.8 us (5%)
  matrix products  24.5 us (5%)
  between operations  13.9 us (3%)
  other arithmetic  8.4 us (2%)
    psum x1, waiting for transfers between devices, per_device(): lax.psum(stacked, 'row').astype(jnp.float32).astype(jnp.bfloat16)  150 us
    psum x1, blocking collectives, per_device(): grad_inverse = lax.psum(inverse_term, 'row')  143 us
    all_gather x1, waiting for transfers between devices, per_device(): grad_total = jnp.sum(lax.all_gather(factor_grad, 'col'), 0)  62.4 us
    all_gather x1, waiting for transfers between devices, per_device(): gathered = lax.all_gather(panel_rows, 'col', axis=1, tiled=True)  25.1 us
    unnamed x11, local copies, waits for them, and re-layouts  14.8 us
  transfers between devices with their start and end apart: 3, of which 3 were waited for; matrix products, arithmetic and copies ran while one was open for 6% of the time, Pallas kernels for 0%

profile of v1, /device:TPU:0, one launch (start us, length us, event | category | flops | bytes accessed | tf_op | source)
XLA Modules:
  0.0 452.6 jit_solution(4560713553950819846)
XLA Ops:
  7.2 0.0 copy-start
  7.2 0.0 all-gather.3.cloned.1.call-start
  7.2 1.7 copy.29
  8.9 0.0 all-gather.3.cloned.1.call-update
  9.0 0.0 all-reduce.3.cloned.1.call-start
  9.1 5.2 %copy.30 = bf16[256,8,4,256]{3,1,2,0:T(8,128)(2,1)} copy(bf16[256,8,4,256]{3,2,1,0:T(4,128)(2,1)} %bitcast.76) | data formatting | bytes 8388608
  14.3 25.1 %all-gather.3.cloned.1.call-done = f32[2048,256]{0,1:T(8,128)} async-done(((f32[2048,32]{0,1:T(8,128)}), f32[2048,256]{0,1:T(8,128)}) %all-gather.3.cloned.1.call-update) | async-done | bytes 2097168 | tf_op jit(solution)/shard_map/all_gather | solution.py:21
  39.4 0.0 copy-done
  39.4 5.0 %convolution_convert_fusion = bf16[2048,256]{1,0:T(8,128)(2,1)S(1)} fusion(f32[2048,256]{0,1:T(8,128)} %all-gather.3.cloned.1.call-done, f32[256,256]{1,0:T(8,128)S(1)} %copy-done), kind=kOutput, calls=%fused_computation.2 | convolution fusion | flops 1611137024 | bytes 3407872 | tf_op jit(solution)/shard_map/dot_general | solution.py:22
  44.4 4.3 fusion.1
  48.8 0.9 pad_maximum_fusion
  49.6 0.0 all-reduce.3.cloned.1.call-update
  49.7 0.2 all-gather.5.cloned.1.call-start
  49.9 150.0 %all-reduce.3.cloned.1.call-done = (bf16[1024,256]{1,0:T(8,128)(2,1)}, bf16[1024,256]{0,1:T(8,128)(2,1)}) async-done(((bf16[1024,256]{1,0:T(8,128)(2,1)}, bf16[1024,256]{0,1:T(8,128)(2,1)}), (bf16[1024,256]{1,0:T(8,128)(2,1)}, bf16[1024,256]{0,1:T(8,128)(2,1)})) %all-reduce.3.cloned.1.call-update) | async-done | bytes 1048592 | tf_op jit(solution)/shard_map/psum | solution.py:34
  199.9 3.7 convolution_negate_fusion
  203.5 0.0 copy-start.3
  203.6 0.2 copy.33
  203.7 0.9 copy-done.3
  204.6 0.1 convert_element_type.29
  204.7 0.1 fusion.13
  204.8 0.1 fusion.10
  204.8 0.1 fusion.7
  204.9 0.1 fusion.4
  205.0 1.8 copy.22
  206.8 0.0 all-gather.5.cloned.1.call-update
  206.8 0.0 copy-start.2
  206.8 7.0 %copy.28 = f32[256,8,4,256]{3,1,2,0:T(8,128)} copy(bf16[256,8,4,256]{3,2,1,0:T(4,128)(2,1)} %bitcast.75) | data formatting | bytes 12582912
  213.8 0.0 copy-done.2
  213.8 7.6 %subtract_convert_fusion = bf16[2048,1024]{1,0:T(8,128)(2,1)} fusion(f32[2048,1024]{1,0:T(8,128)} %bitcast.70, bf16[2048,256]{1,0:T(8,128)(2,1)S(1)} %convolution_convert_fusion, bf16[1024,256]{1,0:T(8,128)(2,1)S(1)} %copy-done.2), kind=kOutput, calls=%fused_computation | convolution fusion | flops 1077936128 | bytes 14155776 | tf_op jit(solution)/shard_map/dot_general | solution.py:36
  221.4 8.0 %reshape.37 = bf16[8,1,256,4,1,256]{5,3,2,0,4,1:T(4,128)(2,1)} reshape(bf16[2048,1024]{1,0:T(8,128)(2,1)} %subtract_convert_fusion) | data formatting | bytes 8388608 | tf_op jit(solution)/shard_map/reshape | solution.py:66
  229.4 0.0 copy-start.1
  229.4 62.4 %all-gather.5.cloned.1.call-done = f32[8,2048,256]{2,1,0:T(8,128)} async-done(((f32[1,2048,256]{2,1,0:T(8,128)}), f32[8,2048,256]{2,1,0:T(8,128)}) %all-gather.5.cloned.1.call-update) | async-done | bytes 16777232 | tf_op jit(solution)/shard_map/all_gather | solution.py:57
  291.8 7.1 %reduce_sum.9 = f32[2048,256]{1,0:T(8,128)S(1)} reduce(f32[8,2048,256]{2,1,0:T(8,128)} %all-gather.5.cloned.1.call-done, f32[]{:T(128)} %constant.125.clone.1), dimensions={0}, to_apply=%region_2.3 | reduce | flops 3670016 | bytes 18874372 | tf_op jit(solution)/shard_map/reduce_sum | solution.py:57
  298.9 0.0 copy-done.1
  298.9 1.2 fusion.17
  300.1 143.2 %psum.23 = f32[256,32]{0,1:T(8,128)} all-reduce(f32[256,32]{0,1:T(8,128)S(1)} %fusion.17), channel_id=1, replica_groups=mesh['row'=32,'col'=8] {'row'}, use_global_device_ids=true, to_apply=%region_3.4 | all-reduce | flops 8192 | bytes 65536 | tf_op jit(solution)/shard_map/psum | solution.py:65
  443.3 2.8 convolution_bitcast_fusion
  (1 shorter events, 0.0 us)
Async XLA Ops:
  7.2 32.2 %copy-start = (f32[256,256]{1,0:T(8,128)S(1)}, f32[256,256]{1,0:T(8,128)}, u32[]{:S(2)}) copy-start(f32[256,256]{1,0:T(8,128)} %param.7) | copy-start | bytes 786436
  7.2 32.2 %all-gather.3.cloned.1.call-start = ((), (), s32[]{:S(2)}) async-start(), calls=%async_computation | async-start | bytes 2359296 | tf_op jit(solution)/shard_map/all_gather | solution.py:21
  9.0 190.9 %all-reduce.3.cloned.1.call-start = ((), (), s32[]{:S(2)}) async-start(), calls=%async_computation.2 | async-start | bytes 2097152 | tf_op jit(solution)/shard_map/psum | solution.py:34
  49.7 242.1 %all-gather.5.cloned.1.call-start = ((), (), s32[]{:S(2)}) async-start(), calls=%async_computation.1 | async-start | bytes 18874368 | tf_op jit(solution)/shard_map/all_gather | solution.py:57
  203.5 1.0 copy-start.3
  206.8 7.0 %copy-start.2 = (bf16[1024,256]{1,0:T(8,128)(2,1)S(1)}, bf16[1024,256]{1,0:T(8,128)(2,1)}, u32[]{:S(2)}) copy-start(bf16[1024,256]{1,0:T(8,128)(2,1)} %get-tuple-element.12) | copy-start | bytes 1572868
  229.4 69.5 %copy-start.1 = (f32[4,8,8,256]{3,1,2,0:T(8,128)S(1)}, f32[4,8,8,256]{3,1,2,0:T(8,128)}, u32[]{:S(2)}) copy-start(f32[4,8,8,256]{3,1,2,0:T(8,128)} %copy.29) | copy-start | bytes 786436
Sparse Core Ops, SparseCore 0:
  10.4 28.9 all-gather.2
  49.8 150.0 all-reduce.2
  207.0 84.7 all-gather.4
